TPU v7x, 512 devices: a whole 4x8x8 slice. The times are simulated.
512 devices in a mesh: chan: 32 (over y, x), row: 16 (over z, core).
Axes of the slice: x: 4, y: 8, z: 8, core: 2. Of those that a mesh axis runs over, the one named last changes fastest.
Arguments:
- amplitudes: bfloat16 [32, 3072, 2048], P('chan', 'row'), may hold values from -6 to 6
- interaction: bfloat16 [32, 2048, 2048], P('chan', 'row'), as said below
- weights6j: float32 [32, 2048], P('chan'), may hold values from -1.5 to 1.5
- column_order: int32 [32, 2048], P('chan'), may hold values from 0 to 2047, each once within a row
- row_counts: int32 [32], P('chan'), may hold values from 768 to 3072, as said below
Outputs:
- pp_update: bfloat16 [32, 3072, 2048], P('chan', 'row')
Inputs may be any that keep to these rules, and one draw needn't show every extreme that they name: Each channel's interaction block is symmetric. `row_counts`: some channel has all 3072 rows live and some channel exactly 768 in every draw.
All inputs are finite; a program needn't handle non-finite values.
Results may differ from a plain program's by a relative error of at most 0.005.
Values may be sent and summed in bfloat16 or wider, within the bound.
No kernel may reach another device: no remote copies, remote signals or barrier semaphores. Data moves between devices by JAX's collectives and lax.ppermute only.
A program may use at most 64 MiB of HBM per device.

v0:
```python
import jax
import jax.numpy as jnp
from jax import lax
from jax.sharding import PartitionSpec as P


def per_device(amplitudes, interaction, weights6j, column_order, row_counts):
    own_block = amplitudes[0]
    row_count = own_block.shape[0]
    col_count = own_block.shape[1]
    v_panel = interaction[0]
    col_order = column_order[0]
    col_weight = weights6j[0]
    gathered = lax.all_to_all(own_block, "chan", split_axis=1, concat_axis=1, tiled=True)
    row_start = lax.axis_index("row") * row_count
    live_rows = row_start + jnp.arange(row_count, dtype=jnp.int32) < row_counts[0]
    taken = jnp.take(gathered, col_order, axis=1).astype(jnp.float32) * col_weight[None, :]
    recoupled = jnp.where(live_rows[:, None], taken, jnp.float32(0.0)).astype(jnp.bfloat16)
    product = jnp.dot(
        recoupled,
        lax.all_gather(v_panel, "row", axis=0, tiled=True),
        preferred_element_type=jnp.float32,
    )
    scaled = (product * col_weight[None, :]).astype(jnp.bfloat16)
    inverse = (
        jnp.zeros((col_count,), jnp.int32).at[col_order].set(jnp.arange(col_count, dtype=jnp.int32))
    )
    restored = jnp.take(scaled, inverse, axis=1)
    returned = lax.all_to_all(restored, "chan", split_axis=1, concat_axis=1, tiled=True)
    return returned[None]


def solution(mesh):
    in_specs = (
        P("chan", "row", None),
        P("chan", "row", None),
        P("chan", None),
        P("chan", None),
        P("chan"),
    )
    out_specs = P("chan", "row", None)
    return jax.shard_map(
        per_device, mesh=mesh, in_specs=in_specs, out_specs=out_specs, check_vma=False
    )
```

profile of v0, /device:TPU:2, one launch (start us, length us, event | category | flops | bytes accessed | tf_op | source)
XLA Modules:
  0.0 133.4 jit_solution(3425176206983938947)
XLA Ops:
  6.5 0.0 all-gather.3.cloned.1.call-start
  6.5 0.7 all-gather.3.cloned.1.call-update
  7.3 0.0 copy-start
  7.3 2.3 %copy.10 = bf16[1,192,2048]{1,2,0:T(8,128)(2,1)} copy(bf16[1,192,2048]{2,1,0:T(8,128)(2,1)} %param.7) | data formatting | bytes 1572864 | tf_op args[0]
  9.5 10.2 %all-to-all-start = ((bf16[192,32,64]{0,2,1:T(8,128)(2,1)}), bf16[192,32,64]{0,2,1:T(8,128)(2,1)S(1)}, u32[]{:S(2)}, u32[]{:S(2)}) async-start(bf16[192,32,64]{0,2,1:T(8,128)(2,1)} %bitcast.4), calls=%async_computation | async-start | bytes 2097152 | tf_op jit(solution)/shard_map/all_to_all | solution.py:14
  20.4 0.0 copy-done
  20.5 8.0 %scatter_custom_fusion = s32[2048]{0:T(1024)S(1)} fusion(s32[2048]{0:T(1024)S(1)} %bitcast.30, s32[2048]{0:T(1024)S(1)} %iota.9, s32[]{:T(128)} %constant.4.clone.1), kind=kCustom, calls=%fused_computation.23 | custom fusion | bytes 8196 | tf_op jit(solution)/shard_map/scatter | solution.py:26
  28.6 19.2 %all-to-all-done = bf16[192,32,64]{0,2,1:T(8,128)(2,1)S(1)} async-done(((bf16[192,32,64]{0,2,1:T(8,128)(2,1)}), bf16[192,32,64]{0,2,1:T(8,128)(2,1)S(1)}, u32[]{:S(2)}, u32[]{:S(2)}) %all-to-all-start) | async-done | bytes 786464 | tf_op jit(solution)/shard_map/all_to_all | solution.py:14
  47.8 7.5 %gather_fusion = bf16[2048,192]{1,0:T(8,128)(2,1)S(1)} fusion(bf16[192,2048]{0,1:T(8,128)(2,1)S(1)} %bitcast.25, s32[2048]{0:T(1024)S(1)} %fusion.15), kind=kCustom, calls=%fused_computation.clone | custom fusion | bytes 1581056 | tf_op jit(solution)/shard_map/jit(_take)/gather | solution.py:17
  55.3 0.0 copy-start.1
  55.4 0.5 copy.11
  55.9 17.6 %all-gather.3.cloned.1.call-done = bf16[1,2048,2048]{2,1,0:T(8,128)(2,1)} async-done(((bf16[1,128,2048]{2,1,0:T(8,128)(2,1)}), bf16[1,2048,2048]{2,1,0:T(8,128)(2,1)}) %all-gather.3.cloned.1.call-update) | async-done | bytes 8388624 | tf_op jit(solution)/shard_map/all_gather | solution.py:21
  73.5 0.0 copy-done.1
  73.5 5.2 %fusion.5 = bf16[192,2048]{1,0:T(8,128)(2,1)S(1)} fusion(bf16[1,2048,2048]{2,1,0:T(8,128)(2,1)} %all-gather.3.cloned.1.call-done, bf16[2048,192]{0,1:T(8,128)(2,1)S(1)} %copy.11, f32[2048]{0:T(1024)S(1)} %bitcast.31, pred[192]{0:T(512)(128)(4,1)S(1)} %add_compare_fusion, pred[2048]{0:T(1024)(128)(4,1)S(1)} %compare_and_fusion.1), kind=kOutput, calls=%fused_computation.6 | convolution fusion | flops 1613365248 | bytes 9971904 | tf_op jit(solution)/shard_map/dot_general | solution.py:19
  78.7 0.5 copy.12
  79.3 7.5 %gather_fusion.1 = bf16[2048,192]{1,0:T(8,128)(2,1)S(1)} fusion(bf16[192,2048]{0,1:T(8,128)(2,1)S(1)} %copy.12, s32[2048]{0:T(1024)S(1)} %fusion.16), kind=kCustom, calls=%fused_computation.1.clone | custom fusion | bytes 1581056 | tf_op jit(solution)/shard_map/jit(_take)/gather | solution.py:28
  86.8 0.4 broadcast_select_fusion
  87.2 38.1 %all_to_all.21 = bf16[192,32,64]{0,2,1:T(8,128)(2,1)S(1)} all-to-all(bf16[192,32,64]{0,2,1:T(8,128)(2,1)S(1)} %bitcast.26), channel_id=1, replica_groups=mesh['chan'=32,'row'=16] {'chan'}, dimensions={1} | all-to-all | bytes 1572864 | tf_op jit(solution)/shard_map/all_to_all | solution.py:29
  125.4 1.2 copy.13
  (7 shorter events, 0.1 us)
Async XLA Ops:
  6.5 67.0 %all-gather.3.cloned.1.call-start = ((), (), s32[]{:S(2)}) async-start(), calls=%async_computation.2 | async-start | bytes 8912896 | tf_op jit(solution)/shard_map/all_gather | solution.py:21
  7.3 13.2 %copy-start = (s32[1,2048]{1,0:T(1,128)S(1)}, s32[1,2048]{1,0:T(1,128)}, u32[]{:S(2)}) copy-start(s32[1,2048]{1,0:T(1,128)} %param.10) | copy-start | bytes 24580
  9.5 38.3 %all-to-all-start = ((bf16[192,32,64]{0,2,1:T(8,128)(2,1)}), bf16[192,32,64]{0,2,1:T(8,128)(2,1)S(1)}, u32[]{:S(2)}, u32[]{:S(2)}) async-start(bf16[192,32,64]{0,2,1:T(8,128)(2,1)} %bitcast.4), calls=%async_computation | async-start | bytes 2097152 | tf_op jit(solution)/shard_map/all_to_all | solution.py:14
  55.3 18.1 %copy-start.1 = (f32[1,2048]{1,0:T(1,128)S(1)}, f32[1,2048]{1,0:T(1,128)}, u32[]{:S(2)}) copy-start(f32[1,2048]{1,0:T(1,128)} %param.9) | copy-start | bytes 24580
Sparse Core Ops, SparseCore 0:
  9.5 63.9 all-gather.2
where the time goes:
time: 134 us; the launch traced here: 133 us
  blocking collectives  38.1 us (28%)
  waiting for transfers between devices  37.6 us (28%)
  local copies, waits for them, and re-layouts  27.6 us (21%)
  between operations  14.2 us (11%)
  starting transfers between devices  10.2 us (8%)
  matrix products  5.23 us (4%)
    all_to_all x1, blocking collectives, per_device(): lax.all_to_all(restored, 'chan', split_axis=1, concat_axis=1, tiled=True)  38.1 us
    all_to_all x1, waiting for transfers between devices, per_device(): lax.all_to_all(own_block, 'chan', split_axis=1, concat_axis=1, tiled=True)  19.2 us
    all_gather x1, waiting for transfers between devices, per_device(): lax.all_gather(v_panel, 'row', axis=0, tiled=True)  17.6 us
    all_to_all x1, starting transfers between devices, per_device(): lax.all_to_all(own_block, 'chan', split_axis=1, concat_axis=1, tiled=True)  10.2 us
    scatter x1, local copies, waits for them, and re-layouts, per_device(): jnp.zeros((col_count,), jnp.int32).at[col_order]  8.05 us
    gather x2, local copies, waits for them, and re-layouts, per_device(): jnp.take(gathered, col_order, axis=1).astype(jnp.float32)  7.99 us
    gather x1, local copies, waits for them, and re-layouts, per_device(): restored = jnp.take(scaled, inverse, axis=1)  7.5 us
    dot_general x1, matrix products, per_device(): jnp.dot(recoupled, lax.all_gather(v_panel, 'row', axis=0, tiled=True), pr...  5.23 us
  transfers between devices with their start and end apart: 2, of which 2 were waited for; matrix products, arithmetic and copies ran while one was open for 14% of the time, Pallas kernels for 0%

commit v1 on v0

--- a/solution.py
+++ b/solution.py
@@ -18,7 +18,9 @@
     recoupled = jnp.where(live_rows[:, None], taken, jnp.float32(0.0)).astype(jnp.bfloat16)
     product = jnp.dot(
         recoupled,
-        lax.all_gather(v_panel, "row", axis=0, tiled=True),
+        jnp.concatenate(
+            lax.all_to_all(jnp.stack([v_panel] * lax.axis_size("row")), "row", 0, 0), axis=0
+        ),
         preferred_element_type=jnp.float32,
     )
     scaled = (product * col_weight[None, :]).astype(jnp.bfloat16)

time: 134 us -> 287 us (2.14)
  waiting for transfers between devices: 37.6 us -> 167 us
  blocking collectives: 38.1 us -> 71.3 us
  between operations: 14.2 us -> 0.79 us
  local copies, waits for them, and re-layouts: 27.6 us -> 31.1 us
    all_to_all x1, waiting for transfers between devices: 19.2 us -> 167 us  [per_device(): lax.all_to_all(jnp.stack([v_panel] * lax.axis_size('row')), 'row', 0, 0)]
    all_to_all x0 -> x1, blocking collectives: none -> 38.1 us  [per_device(): lax.all_to_all(own_block, 'chan', split_axis=1, concat_axis=1, tiled=True)]
    all_gather x1 -> x0, waiting for transfers between devices: 17.6 us -> none  [per_device(): lax.all_gather(v_panel, 'row', axis=0, tiled=True)]
    all_to_all x1, blocking collectives: 38.1 us -> 33.2 us  [per_device(): lax.all_to_all(restored, 'chan', split_axis=1, concat_axis=1, tiled=True)]
    another operation x0 -> x1, local copies, waits for them, and re-layouts: none -> 4.32 us  [per_device(): jnp.stack([v_panel] * lax.axis_size('row'))]
  transfers between devices with their start and end apart: 2 -> 1, of which waited for: 2 -> 1; matrix products, arithmetic and copies ran while one was open for 14% -> 6% of each run, Pallas kernels for 0% -> 0%
where the time goes in v1:
time: 287 us
  waiting for transfers between devices  167 us (58%)
  blocking collectives  71.3 us (25%)
  local copies, waits for them, and re-layouts  31.1 us (11%)
  starting transfers between devices  10.6 us (4%)
  matrix products  5.24 us (2%)
    all_to_all x1, waiting for transfers between devices, per_device(): lax.all_to_all(jnp.stack([v_panel] * lax.axis_size('row')), 'row', 0, 0)  167 us
    all_to_all x1, blocking collectives, per_device(): lax.all_to_all(own_block, 'chan', split_axis=1, concat_axis=1, tiled=True)  38.1 us
    all_to_all x1, blocking collectives, per_device(): lax.all_to_all(restored, 'chan', split_axis=1, concat_axis=1, tiled=True)  33.2 us
    all_to_all x1, starting transfers between devices, per_device(): lax.all_to_all(jnp.stack([v_panel] * lax.axis_size('row')), 'row', 0, 0)  10.6 us
    scatter x1, local copies, waits for them, and re-layouts, per_device(): jnp.zeros((col_count,), jnp.int32).at[col_order]  8.05 us
    gather x2, local copies, waits for them, and re-layouts, per_device(): jnp.take(gathered, col_order, axis=1).astype(jnp.float32)  8 us
    gather x1, local copies, waits for them, and re-layouts, per_device(): restored = jnp.take(scaled, inverse, axis=1)  7.5 us
  transfers between devices with their start and end apart: 1, of which 1 were waited for; matrix products, arithmetic and copies ran while one was open for 6% of the time, Pallas kernels for 0%

profile of v1, /device:TPU:2, one launch (start us, length us, event | category | flops | bytes accessed | tf_op | source)
XLA Modules:
  0.0 287.0 jit_solution(4492723865463700360)
XLA Ops:
  0.0 0.0 copy-start
  0.0 1.5 copy.10
  1.5 38.1 %all_to_all.26 = bf16[192,32,64]{0,2,1:T(8,128)(2,1)S(1)} all-to-all(bf16[192,32,64]{0,2,1:T(8,128)(2,1)S(1)} %bitcast.24), channel_id=1, replica_groups=mesh['chan'=32,'row'=16] {'chan'}, dimensions={1} | all-to-all | bytes 1572864 | tf_op jit(solution)/shard_map/all_to_all | solution.py:14
  39.6 0.0 copy-done
  39.6 4.3 %stack.3 = bf16[16,128,2048]{2,1,0:T(8,128)(2,1)} broadcast(bf16[128,2048]{1,0:T(8,128)(2,1)S(1)} %bitcast.25), dimensions={1,2} | broadcast | bytes 8912896 | tf_op jit(solution)/shard_map/stack | solution.py:22
  43.9 0.0 copy-start.1
  43.9 10.6 %all-to-all-start.1 = ((bf16[16,128,2048]{2,1,0:T(8,128)(2,1)}), bf16[16,128,2048]{2,1,0:T(8,128)(2,1)}, u32[]{:S(2)}, u32[]{:S(2)}) async-start(bf16[16,128,2048]{2,1,0:T(8,128)(2,1)} %stack.3), calls=%async_computation.1 | async-start | bytes 16777216 | tf_op jit(solution)/shard_map/all_to_all | solution.py:22
  55.2 0.0 copy-done.1
  55.2 8.0 %scatter_custom_fusion = s32[2048]{0:T(1024)S(1)} fusion(s32[2048]{0:T(1024)S(1)} %bitcast.28, s32[2048]{0:T(1024)S(1)} %iota.9, s32[]{:T(128)} %constant.4.clone.1), kind=kCustom, calls=%fused_computation.21 | custom fusion | bytes 8196 | tf_op jit(solution)/shard_map/scatter | solution.py:28
  63.4 7.5 %gather_fusion = bf16[2048,192]{1,0:T(8,128)(2,1)S(1)} fusion(bf16[192,2048]{0,1:T(8,128)(2,1)S(1)} %bitcast.21, s32[2048]{0:T(1024)S(1)} %fusion.8), kind=kCustom, calls=%fused_computation.clone | custom fusion | bytes 1581056 | tf_op jit(solution)/shard_map/jit(_take)/gather | solution.py:17
  70.9 0.0 copy-start.2
  70.9 0.5 copy.11
  71.4 167.4 %all-to-all-done.1 = bf16[16,128,2048]{2,1,0:T(8,128)(2,1)} async-done(((bf16[16,128,2048]{2,1,0:T(8,128)(2,1)}), bf16[16,128,2048]{2,1,0:T(8,128)(2,1)}, u32[]{:S(2)}, u32[]{:S(2)}) %all-to-all-start.1) | async-done | bytes 8388640 | tf_op jit(solution)/shard_map/all_to_all | solution.py:22
  238.8 0.0 copy-done.2
  238.8 5.2 %fusion = bf16[192,2048]{1,0:T(8,128)(2,1)S(1)} fusion(bf16[2048,2048]{1,0:T(8,128)(2,1)} %bitcast.9, bf16[2048,192]{0,1:T(8,128)(2,1)S(1)} %copy.11, f32[2048]{0:T(1024)S(1)} %bitcast.29, pred[192]{0:T(512)(128)(4,1)S(1)} %add_compare_fusion, pred[2048]{0:T(1024)(128)(4,1)S(1)} %compare_and_fusion.1), kind=kOutput, calls=%fused_computation.4 | convolution fusion | flops 1613365248 | bytes 9971904 | tf_op jit(solution)/shard_map/dot_general | solution.py:19
  244.0 0.5 copy.12
  244.6 7.5 %gather_fusion.1 = bf16[2048,192]{1,0:T(8,128)(2,1)S(1)} fusion(bf16[192,2048]{0,1:T(8,128)(2,1)S(1)} %copy.12, s32[2048]{0:T(1024)S(1)} %fusion.9), kind=kCustom, calls=%fused_computation.1.clone | custom fusion | bytes 1581056 | tf_op jit(solution)/shard_map/jit(_take)/gather | solution.py:30
  252.1 0.4 broadcast_select_fusion
  252.5 33.2 %all_to_all.27 = bf16[192,32,64]{0,2,1:T(8,128)(2,1)S(1)} all-to-all(bf16[192,32,64]{0,2,1:T(8,128)(2,1)S(1)} %bitcast.22), channel_id=1, replica_groups=mesh['chan'=32,'row'=16] {'chan'}, dimensions={1} | all-to-all | bytes 1572864 | tf_op jit(solution)/shard_map/all_to_all | solution.py:31
  285.8 1.2 copy.13
  (7 shorter events, 0.1 us)
Async XLA Ops:
  0.0 39.6 %copy-start = (bf16[1,128,2048]{2,1,0:T(8,128)(2,1)S(1)}, bf16[1,128,2048]{2,1,0:T(8,128)(2,1)}, u32[]{:S(2)}) copy-start(bf16[1,128,2048]{2,1,0:T(8,128)(2,1)} %param.8) | copy-start | bytes 1572868
  43.9 11.3 %copy-start.1 = (s32[1,2048]{1,0:T(1,128)S(1)}, s32[1,2048]{1,0:T(1,128)}, u32[]{:S(2)}) copy-start(s32[1,2048]{1,0:T(1,128)} %param.10) | copy-start | bytes 24580
  43.9 194.9 %all-to-all-start.1 = ((bf16[16,128,2048]{2,1,0:T(8,128)(2,1)}), bf16[16,128,2048]{2,1,0:T(8,128)(2,1)}, u32[]{:S(2)}, u32[]{:S(2)}) async-start(bf16[16,128,2048]{2,1,0:T(8,128)(2,1)} %stack.3), calls=%async_computation.1 | async-start | bytes 16777216 | tf_op jit(solution)/shard_map/all_to_all | solution.py:22
  70.9 167.9 %copy-start.2 = (f32[1,2048]{1,0:T(1,128)S(1)}, f32[1,2048]{1,0:T(1,128)}, u32[]{:S(2)}) copy-start(f32[1,2048]{1,0:T(1,128)} %param.9) | copy-start | bytes 24580
